TPU v7x, 32 devices: a whole 2x2x4 slice. The times are simulated.
32 devices in a mesh: dp: 4 (over z), ctx: 8 (over y, x, core).
Axes of the slice: x: 2, y: 2, z: 4, core: 2. Of those that a mesh axis runs over, the one named last changes fastest.
Arguments:
- queries: bfloat16 [8192, 4096], P(('dp', 'ctx')), parts along dimension 0, may hold values from -24 to 24
- keys: bfloat16 [8192, 4096], P(('dp', 'ctx')), parts along dimension 0, may hold values from -24 to 24
- values: bfloat16 [8192, 4096], P(('dp', 'ctx')), parts along dimension 0, may hold values from -12 to 12
- mem_keys: bfloat16 [64, 512, 4096], P(('dp', 'ctx')), parts along dimension 0, may hold values from -9 to 9
- mem_values: bfloat16 [64, 512, 4096], P(('dp', 'ctx')), parts along dimension 0, may hold values from -12 to 12
- mem_ids: int32 [128, 2, 2], P('dp'), parts along dimension 0, may hold values from 0 to 15, as said below
Outputs:
- attended: bfloat16 [8192, 4096], P(('dp', 'ctx')), parts along dimension 0
There are 4 independent parts, one for each index of `dp`. A program takes and returns all parts, laid end to end along the dimension named above; each array names one. Nothing has to cross between parts.
Inputs may be any that keep to these rules, and one draw needn't show every extreme that they name: mem_ids[h, t, :] names 2 memory blocks (one block may be named twice). Among the lists of each aligned group of 4 heads, at most 4 entries name blocks of one holder (blocks k * 2 to k * 2 + 1), and in every draw the blocks of some holder are named exactly 4 times by every group.
All inputs are finite; a program needn't handle non-finite values.
Results may differ from a plain program's by a relative error of at most 0.0045.
Values may be sent and summed in bfloat16 or wider, within the bound.
A program may use at most 192 MiB of HBM per device.

v0:
```python
import functools
import math

import jax
import jax.numpy as jnp
from jax import lax
from jax.experimental import pallas as pl
from jax.experimental.pallas import tpu as pltpu
from jax.sharding import PartitionSpec as P

HD = 128
CHUNK = 512
MESH = pl.DeviceIdType.MESH


def entry_tables(mem_ids, devices, device_index, blocks_here, capacity):
    head_count, tile_count, listed = mem_ids.shape
    entries = head_count * tile_count * listed // devices
    per_head = tile_count * listed
    heads_here = head_count // devices
    ids = mem_ids.reshape(devices, entries)
    holder = ids // blocks_here
    position = jnp.arange(entries, dtype=jnp.int32)
    same = holder[:, :, None] == holder[:, None, :]
    earlier = position[None, :] < position[:, None]
    rank = jnp.sum((same & earlier[None]).astype(jnp.int32), axis=2)
    slots = jnp.arange(capacity, dtype=jnp.int32)
    chosen = (holder[:, None, :] == device_index) & (rank[:, None, :] == slots[None, :, None])
    head = jnp.arange(devices, dtype=jnp.int32)[:, None] * heads_here + position[None, :] // per_head
    code = head * blocks_here + ids % blocks_here
    send_table = jnp.sum(jnp.where(chosen, code[:, None, :], 0), axis=2).reshape(-1)
    own = jnp.arange(devices, dtype=jnp.int32)[:, None] == device_index
    receive_table = jnp.sum(jnp.where(own, holder * capacity + rank, 0), axis=0)
    return send_table, receive_table


def kernel(
    devices, capacity, tile_count, listed,
    send_table, receive_table, q_hbm, k_hbm, v_hbm, mk_hbm, mv_hbm, out_hbm,
    q_in, k_in, v_in, store_k, store_v, packed, arrived, out_buf,
    qkv_recv, qkv_send, mem_load, mem_recv, mem_send, out_recv, out_send,
):
    me = lax.axis_index("ctx")
    heads_here, span, _ = q_in.shape
    rows = q_hbm.shape[0]
    blocks_here, block_rows, columns = mk_hbm.shape
    head_count = columns // HD
    tile_rows = span // tile_count
    chunks = span // CHUNK
    peers_per_chunk = CHUNK // rows
    pieces = capacity * 2
    exponent_scale = HD ** (-0.5) * math.log2(math.e)

    def columns_of(head):
        return pl.ds(pl.multiple_of(head * HD, HD), HD)

    def rows_of(device):
        return pl.ds(pl.multiple_of(device * rows, rows), rows)

    def load_head(head, carry):
        for source, target, which in ((mk_hbm, store_k, 0), (mv_hbm, store_v, 1)):
            pltpu.make_async_copy(
                source.at[:, :, columns_of(head)],
                target.at[pl.ds(head * blocks_here, blocks_here)],
                mem_load.at[which],
            ).start()
        return carry

    lax.fori_loop(0, head_count, load_head, 0)

    barrier = pltpu.get_barrier_semaphore()

    def greet(offset, carry):
        pl.semaphore_signal(
            barrier, inc=1, device_id={"ctx": lax.rem(me + offset, devices)}, device_id_type=MESH
        )
        return carry

    lax.fori_loop(1, devices, greet, 0)
    pl.semaphore_wait(barrier, devices - 1)

    def send_head(head, carry):
        def to_peer(offset, inner):
            peer = lax.rem(me + offset, devices)
            for which, (source, target) in enumerate(((q_hbm, q_in), (k_hbm, k_in), (v_hbm, v_in))):
                pltpu.make_async_remote_copy(
                    src_ref=source.at[:, columns_of(peer * heads_here + head)],
                    dst_ref=target.at[head, rows_of(me)],
                    send_sem=qkv_send.at[which],
                    recv_sem=qkv_recv.at[which, head],
                    device_id={"ctx": peer},
                    device_id_type=MESH,
                ).start()
            return inner

        lax.fori_loop(1, devices, to_peer, 0)
        for which, (source, target) in enumerate(((q_hbm, q_in), (k_hbm, k_in), (v_hbm, v_in))):
            pltpu.make_async_copy(
                source.at[:, columns_of(me * heads_here + head)],
                target.at[head, rows_of(me)],
                qkv_recv.at[which, head],
            ).start()
        return carry

    send_head(0, 0)

    pltpu.make_async_copy(store_k, store_k, mem_load.at[0]).wait()
    pltpu.make_async_copy(store_v, store_v, mem_load.at[1]).wait()

    def pieces_of(device):
        return pl.ds(pl.multiple_of(device * pieces, pieces), pieces)

    def pack(device):
        for slot in range(capacity):
            code = send_table[device * capacity + slot]
            packed[device * pieces + 2 * slot] = store_k[code]
            packed[device * pieces + 2 * slot + 1] = store_v[code]

    def send_memory(peer):
        pltpu.make_async_remote_copy(
            src_ref=packed.at[pieces_of(peer)],
            dst_ref=arrived.at[pieces_of(me)],
            send_sem=mem_send,
            recv_sem=mem_recv,
            device_id={"ctx": peer},
            device_id_type=MESH,
        ).start()

    def pack_and_send(offset, carry):
        pack(lax.rem(me + offset + 1, devices))
        send_memory(lax.rem(me + offset, devices))
        return carry

    pack(lax.rem(me + 1, devices))
    lax.fori_loop(1, devices, pack_and_send, 0)
    pltpu.make_async_copy(packed.at[pieces_of(me)], arrived.at[pieces_of(me)], mem_recv).start()

    lax.fori_loop(1, heads_here, send_head, 0)

    def send_output(head, chunk):
        for part in range(peers_per_chunk):
            peer = chunk * peers_per_chunk + part
            source = out_buf.at[head, rows_of(peer)]
            target = out_hbm.at[:, columns_of(me * heads_here + head)]

            @pl.when(peer != me)
            def _():
                pltpu.make_async_remote_copy(
                    src_ref=source,
                    dst_ref=target,
                    send_sem=out_send,
                    recv_sem=out_recv,
                    device_id={"ctx": peer},
                    device_id_type=MESH,
                ).start()

            @pl.when(peer == me)
            def _():
                pltpu.make_async_copy(source, target, out_recv).start()

    pltpu.make_async_copy(arrived, arrived, mem_recv).wait()

    def absorb(queries, block_keys, block_values, state, masked):
        running_max, weight_sum, numerator = state
        scores = lax.dot_general(
            queries, block_keys, (((1,), (1,)), ((), ())), preferred_element_type=jnp.float32
        )
        if masked:
            row = lax.broadcasted_iota(jnp.int32, scores.shape, 0)
            column = lax.broadcasted_iota(jnp.int32, scores.shape, 1)
            scores = jnp.where(row >= column, scores, -jnp.inf)
        new_max = jnp.maximum(running_max, jnp.max(scores, axis=1, keepdims=True))
        rescale = jnp.exp2((running_max - new_max) * exponent_scale)
        weights = jnp.exp2((scores - new_max) * exponent_scale)
        weight_sum = weight_sum * rescale + jnp.sum(weights, axis=1, keepdims=True)
        numerator = numerator * rescale + jnp.dot(
            weights.astype(jnp.bfloat16), block_values, preferred_element_type=jnp.float32
        )
        return new_max, weight_sum, numerator

    def one_head(head, carry):
        for which, target in enumerate((q_in, k_in, v_in)):
            pltpu.make_async_copy(
                target.at[head], target.at[head], qkv_recv.at[which, head]
            ).wait()

        def one_chunk(chunk, inner):
            chunk_rows = pl.ds(pl.multiple_of(chunk * CHUNK, CHUNK), CHUNK)
            queries = q_in[head, chunk_rows]
            tile = chunk * CHUNK // tile_rows
            state = (
                jnp.full((CHUNK, 1), -jnp.inf, jnp.float32),
                jnp.zeros((CHUNK, 1), jnp.float32),
                jnp.zeros((CHUNK, HD), jnp.float32),
            )
            state = absorb(queries, k_in[head, chunk_rows], v_in[head, chunk_rows], state, True)
            for slot in range(listed):
                piece = receive_table[(head * tile_count + tile) * listed + slot] * 2
                state = absorb(queries, arrived[piece], arrived[piece + 1], state, False)

            def earlier(block, current):
                block_at = pl.ds(pl.multiple_of(block * CHUNK, CHUNK), CHUNK)
                return absorb(queries, k_in[head, block_at], v_in[head, block_at], current, False)

            _, weight_sum, numerator = lax.fori_loop(0, chunk, earlier, state)
            out_buf[head, chunk_rows] = (numerator / weight_sum).astype(jnp.bfloat16)

            @pl.when(chunk > 0)
            def _():
                send_output(head, chunk - 1)

            @pl.when((chunk == 0) & (head > 0))
            def _():
                send_output(head - 1, chunks - 1)

            return inner

        lax.fori_loop(0, chunks, one_chunk, 0)
        return carry

    lax.fori_loop(0, heads_here, one_head, 0)

    others = pl.ds(0, (devices - 1) * rows)
    for which, target in enumerate((q_in, k_in, v_in)):
        sent = target.at[:, others]
        pltpu.make_async_copy(sent, sent, qkv_send.at[which]).wait()
    sent = packed.at[pl.ds(0, (devices - 1) * pieces)]
    pltpu.make_async_copy(sent, sent, mem_send).wait()
    send_output(heads_here - 1, chunks - 1)
    sent = out_buf.at[:, others]
    pltpu.make_async_copy(sent, sent, out_send).wait()
    pltpu.make_async_copy(out_hbm, out_hbm, out_recv).wait()


def shards(queries, keys, values, mem_keys, mem_values, mem_ids):
    devices = lax.axis_size("ctx")
    device_index = lax.axis_index("ctx")
    head_count, tile_count, listed = mem_ids.shape
    heads_here = head_count // devices
    blocks_here, block_rows, columns = mem_keys.shape
    rows = queries.shape[0]
    span = rows * devices
    capacity = max(2, 2 * heads_here * tile_count * listed // devices)
    send_table, receive_table = entry_tables(
        mem_ids, devices, device_index, blocks_here, capacity
    )
    store = pltpu.VMEM((head_count * blocks_here, block_rows, HD), jnp.bfloat16)
    exchange = pltpu.VMEM((devices * capacity * 2, block_rows, HD), jnp.bfloat16)
    head_rows = pltpu.VMEM((heads_here, span, HD), jnp.bfloat16)
    anywhere = pl.BlockSpec(memory_space=pl.ANY)
    table = pl.BlockSpec(memory_space=pltpu.SMEM)
    return pl.pallas_call(
        functools.partial(kernel, devices, capacity, tile_count, listed),
        out_shape=jax.ShapeDtypeStruct((rows, columns), jnp.bfloat16),
        in_specs=[table, table] + [anywhere] * 5,
        out_specs=anywhere,
        scratch_shapes=[
            head_rows, head_rows, head_rows, store, store, exchange, exchange, head_rows,
            pltpu.SemaphoreType.DMA((3, heads_here)),
            pltpu.SemaphoreType.DMA((3,)),
            pltpu.SemaphoreType.DMA((2,)),
            pltpu.SemaphoreType.DMA,
            pltpu.SemaphoreType.DMA,
            pltpu.SemaphoreType.DMA,
            pltpu.SemaphoreType.DMA,
        ],
        compiler_params=pltpu.CompilerParams(
            collective_id=0, has_side_effects=True, vmem_limit_bytes=64_000_000
        ),
        name="exchange_attention",
    )(send_table, receive_table, queries, keys, values, mem_keys, mem_values)


def solution(mesh):
    in_specs = (
        P(("dp", "ctx"), None),
        P(("dp", "ctx"), None),
        P(("dp", "ctx"), None),
        P(("dp", "ctx"), None, None),
        P(("dp", "ctx"), None, None),
        P("dp", None, None),
    )
    out_specs = P(("dp", "ctx"), None)
    return jax.shard_map(shards, mesh=mesh, in_specs=in_specs, out_specs=out_specs, check_vma=False)
```

profile of v0, /device:TPU:1, one launch (start us, length us, event | category | flops | bytes accessed | tf_op | source)
XLA Modules:
  0.0 192.0 jit_solution(12041672589502660489)
XLA Ops:
  0.0 0.8 copy.9
  0.8 0.1 reshape.179
  0.9 0.1 fusion.1
  1.0 0.3 convert_reduce_fusion
  1.3 0.6 select_reduce_fusion.1.receive_table
  1.9 0.1 select_reduce_fusion
  2.0 0.1 copy.10
  2.1 0.6 reshape.180.send_table
  2.7 186.1 %exchange_attention.1 = bf16[256,4096]{1,0:T(8,128)(2,1)} custom-call(s32[32]{0:T(128)} %reshape.180.send_table, s32[16]{0:T(128)} %select_reduce_fusion.1.receive_table, bf16[256,4096]{1,0:T(8,128)(2,1)} %q_hbm.1, bf16[256,4096]{1,0:T(8,128)(2,1)} %k_hbm.1, bf16[256,4096]{1,0:T(8,128)(2,1)} %v_hbm.1, bf16[2,512,4096]{2,1,0:T(8,128)(2,1)} %mk_hbm.1, ...), custom_call_target="tpu_custom_call" | custom-call | tf_op jit(solution)/shard_map/exchange_attention/pallas_call | solution.py:252
  188.8 3.1 %copy.12 = bf16[256,4096]{1,0:T(8,128)(2,1)} copy(bf16[256,4096]{1,0:T(8,128)(2,1)} %exchange_attention.1) | data formatting | bytes 4194304
  (5 shorter events, 0.0 us)
where the time goes:
time: 192 us
  Pallas kernels  186 us (97%)
  local copies, waits for them, and re-layouts  4.7 us (2%)
    pallas_call x1, Pallas kernels, shards(): pl.pallas_call(functools.partial(kernel, devices, capacity, tile_count, l...  186 us
    unnamed x2, local copies, waits for them, and re-layouts  3.91 us

commit v1 on v0

--- a/solution.py
+++ b/solution.py
@@ -13,34 +13,14 @@
 MESH = pl.DeviceIdType.MESH
 
 
-def entry_tables(mem_ids, devices, device_index, blocks_here, capacity):
-    head_count, tile_count, listed = mem_ids.shape
-    entries = head_count * tile_count * listed // devices
-    per_head = tile_count * listed
-    heads_here = head_count // devices
-    ids = mem_ids.reshape(devices, entries)
-    holder = ids // blocks_here
-    position = jnp.arange(entries, dtype=jnp.int32)
-    same = holder[:, :, None] == holder[:, None, :]
-    earlier = position[None, :] < position[:, None]
-    rank = jnp.sum((same & earlier[None]).astype(jnp.int32), axis=2)
-    slots = jnp.arange(capacity, dtype=jnp.int32)
-    chosen = (holder[:, None, :] == device_index) & (rank[:, None, :] == slots[None, :, None])
-    head = jnp.arange(devices, dtype=jnp.int32)[:, None] * heads_here + position[None, :] // per_head
-    code = head * blocks_here + ids % blocks_here
-    send_table = jnp.sum(jnp.where(chosen, code[:, None, :], 0), axis=2).reshape(-1)
-    own = jnp.arange(devices, dtype=jnp.int32)[:, None] == device_index
-    receive_table = jnp.sum(jnp.where(own, holder * capacity + rank, 0), axis=0)
-    return send_table, receive_table
-
-
 def kernel(
-    devices, capacity, tile_count, listed,
-    send_table, receive_table, q_hbm, k_hbm, v_hbm, mk_hbm, mv_hbm, out_hbm,
+    devices, capacity,
+    ids, q_hbm, k_hbm, v_hbm, mk_hbm, mv_hbm, out_hbm,
     q_in, k_in, v_in, store_k, store_v, packed, arrived, out_buf,
     qkv_recv, qkv_send, mem_load, mem_recv, mem_send, out_recv, out_send,
 ):
     me = lax.axis_index("ctx")
+    tile_count, listed, _ = ids.shape
     heads_here, span, _ = q_in.shape
     rows = q_hbm.shape[0]
     blocks_here, block_rows, columns = mk_hbm.shape
@@ -49,6 +29,8 @@
     chunks = span // CHUNK
     peers_per_chunk = CHUNK // rows
     pieces = capacity * 2
+    per_head = tile_count * listed
+    entries = heads_here * per_head
     exponent_scale = HD ** (-0.5) * math.log2(math.e)
 
     def columns_of(head):
@@ -110,11 +92,35 @@
     def pieces_of(device):
         return pl.ds(pl.multiple_of(device * pieces, pieces), pieces)
 
+    def listed_block(group, entry):
+        head = group * heads_here + lax.div(entry, per_head)
+        return head, ids[lax.div(lax.rem(entry, per_head), listed), lax.rem(entry, listed), head]
+
     def pack(device):
-        for slot in range(capacity):
-            code = send_table[device * capacity + slot]
+        def look(entry, found):
+            count, codes = found
+            head, block = listed_block(device, entry)
+            mine = lax.div(block, blocks_here) == me
+            code = head * blocks_here + lax.rem(block, blocks_here)
+            codes = tuple(
+                jnp.where(mine & (count == slot), code, held) for slot, held in enumerate(codes)
+            )
+            return count + jnp.where(mine, 1, 0), codes
+
+        zero = jnp.int32(0)
+        _, codes = lax.fori_loop(0, entries, look, (zero, (zero,) * capacity))
+        for slot, code in enumerate(codes):
             packed[device * pieces + 2 * slot] = store_k[code]
             packed[device * pieces + 2 * slot + 1] = store_v[code]
+
+    def piece_of(entry):
+        holder = lax.div(listed_block(me, entry)[1], blocks_here)
+
+        def look(other, rank):
+            same = lax.div(listed_block(me, other)[1], blocks_here) == holder
+            return rank + jnp.where(same, 1, 0)
+
+        return (holder * capacity + lax.fori_loop(0, entry, look, jnp.int32(0))) * 2
 
     def send_memory(peer):
         pltpu.make_async_remote_copy(
@@ -184,10 +190,11 @@
                 target.at[head], target.at[head], qkv_recv.at[which, head]
             ).wait()
 
-        def one_chunk(chunk, inner):
+        def one_chunk(step, inner):
+            chunk = step
             chunk_rows = pl.ds(pl.multiple_of(chunk * CHUNK, CHUNK), CHUNK)
             queries = q_in[head, chunk_rows]
-            tile = chunk * CHUNK // tile_rows
+            tile = lax.div(chunk * CHUNK, tile_rows)
             state = (
                 jnp.full((CHUNK, 1), -jnp.inf, jnp.float32),
                 jnp.zeros((CHUNK, 1), jnp.float32),
@@ -195,7 +202,7 @@
             )
             state = absorb(queries, k_in[head, chunk_rows], v_in[head, chunk_rows], state, True)
             for slot in range(listed):
-                piece = receive_table[(head * tile_count + tile) * listed + slot] * 2
+                piece = piece_of((head * tile_count + tile) * listed + slot)
                 state = absorb(queries, arrived[piece], arrived[piece + 1], state, False)
 
             def earlier(block, current):
@@ -205,11 +212,11 @@
             _, weight_sum, numerator = lax.fori_loop(0, chunk, earlier, state)
             out_buf[head, chunk_rows] = (numerator / weight_sum).astype(jnp.bfloat16)
 
-            @pl.when(chunk > 0)
+            @pl.when(step > 0)
             def _():
-                send_output(head, chunk - 1)
-
-            @pl.when((chunk == 0) & (head > 0))
+                send_output(head, step - 1)
+
+            @pl.when((step == 0) & (head > 0))
             def _():
                 send_output(head - 1, chunks - 1)
 
@@ -232,27 +239,27 @@
     pltpu.make_async_copy(out_hbm, out_hbm, out_recv).wait()
 
 
+def hand_over(source_ref, target_ref):
+    target_ref[...] = source_ref[...]
+
+
 def shards(queries, keys, values, mem_keys, mem_values, mem_ids):
     devices = lax.axis_size("ctx")
-    device_index = lax.axis_index("ctx")
     head_count, tile_count, listed = mem_ids.shape
     heads_here = head_count // devices
     blocks_here, block_rows, columns = mem_keys.shape
     rows = queries.shape[0]
     span = rows * devices
     capacity = max(2, 2 * heads_here * tile_count * listed // devices)
-    send_table, receive_table = entry_tables(
-        mem_ids, devices, device_index, blocks_here, capacity
-    )
     store = pltpu.VMEM((head_count * blocks_here, block_rows, HD), jnp.bfloat16)
     exchange = pltpu.VMEM((devices * capacity * 2, block_rows, HD), jnp.bfloat16)
     head_rows = pltpu.VMEM((heads_here, span, HD), jnp.bfloat16)
     anywhere = pl.BlockSpec(memory_space=pl.ANY)
     table = pl.BlockSpec(memory_space=pltpu.SMEM)
-    return pl.pallas_call(
-        functools.partial(kernel, devices, capacity, tile_count, listed),
+    attended = pl.pallas_call(
+        functools.partial(kernel, devices, capacity),
         out_shape=jax.ShapeDtypeStruct((rows, columns), jnp.bfloat16),
-        in_specs=[table, table] + [anywhere] * 5,
+        in_specs=[table] + [anywhere] * 5,
         out_specs=anywhere,
         scratch_shapes=[
             head_rows, head_rows, head_rows, store, store, exchange, exchange, head_rows,
@@ -268,7 +275,16 @@
             collective_id=0, has_side_effects=True, vmem_limit_bytes=64_000_000
         ),
         name="exchange_attention",
-    )(send_table, receive_table, queries, keys, values, mem_keys, mem_values)
+    )(mem_ids.transpose(1, 2, 0), queries, keys, values, mem_keys, mem_values)
+    block = pl.BlockSpec((rows // 4, columns), lambda step: (step, 0))
+    return pl.pallas_call(
+        hand_over,
+        out_shape=jax.ShapeDtypeStruct((rows, columns), jnp.bfloat16),
+        grid=(4,),
+        in_specs=[block],
+        out_specs=block,
+        name="hand_over",
+    )(attended)
 
 
 def solution(mesh):

time: 192 us -> 190 us (0.990)
  local copies, waits for them, and re-layouts: 4.7 us -> 0 us
  Pallas kernels: 186 us -> 190 us
    unnamed x2 -> x0, local copies, waits for them, and re-layouts: 3.91 us -> none
    pallas_call x1 -> x2, Pallas kernels: 186 us -> 190 us  [the longest x1 186 us: shards(): pl.pallas_call(functools.partial(kernel, devices, capacity), out_shape=ja...]
where the time goes in v1:
time: 190 us
  Pallas kernels  190 us (100%)
    pallas_call x1, Pallas kernels, shards(): pl.pallas_call(functools.partial(kernel, devices, capacity), out_shape=ja...  186 us

profile of v1, /device:TPU:1, one launch (start us, length us, event | category | flops | bytes accessed | tf_op | source)
XLA Modules:
  0.0 189.9 jit_solution(4462443041473549297)
XLA Ops:
  0.0 186.1 %exchange_attention.1.source_ref = bf16[256,4096]{1,0:T(8,128)(2,1)} custom-call(s32[2,2,32]{2,1,0:T(2,128)} %bitcast.1, bf16[256,4096]{1,0:T(8,128)(2,1)} %q_hbm.1, bf16[256,4096]{1,0:T(8,128)(2,1)} %k_hbm.1, bf16[256,4096]{1,0:T(8,128)(2,1)} %v_hbm.1, bf16[2,512,4096]{2,1,0:T(8,128)(2,1)} %mk_hbm.1, bf16[2,512,4096]{2,1,0:T(8,128)(2,1)} %mv_hbm.1), custom_call_target="tpu_custom_call" | custom-call | tf_op jit(solution)/shard_map/exchange_attention/pallas_call | solution.py:259
  186.1 3.8 %hand_over.1 = bf16[256,4096]{1,0:T(8,128)(2,1)} custom-call(bf16[256,4096]{1,0:T(8,128)(2,1)} %exchange_attention.1.source_ref), custom_call_target="tpu_custom_call" | custom-call | tf_op jit(solution)/shard_map/hand_over/pallas_call | solution.py:280

commit v2 on v1

--- a/solution.py
+++ b/solution.py
@@ -239,10 +239,6 @@
     pltpu.make_async_copy(out_hbm, out_hbm, out_recv).wait()
 
 
-def hand_over(source_ref, target_ref):
-    target_ref[...] = source_ref[...]
-
-
 def shards(queries, keys, values, mem_keys, mem_values, mem_ids):
     devices = lax.axis_size("ctx")
     head_count, tile_count, listed = mem_ids.shape
@@ -256,11 +252,11 @@
     head_rows = pltpu.VMEM((heads_here, span, HD), jnp.bfloat16)
     anywhere = pl.BlockSpec(memory_space=pl.ANY)
     table = pl.BlockSpec(memory_space=pltpu.SMEM)
-    attended = pl.pallas_call(
+    return pl.pallas_call(
         functools.partial(kernel, devices, capacity),
-        out_shape=jax.ShapeDtypeStruct((rows, columns), jnp.bfloat16),
+        out_shape=pltpu.VMEM((rows, columns), jnp.bfloat16),
         in_specs=[table] + [anywhere] * 5,
-        out_specs=anywhere,
+        out_specs=pl.BlockSpec(memory_space=pltpu.VMEM),
         scratch_shapes=[
             head_rows, head_rows, head_rows, store, store, exchange, exchange, head_rows,
             pltpu.SemaphoreType.DMA((3, heads_here)),
@@ -272,19 +268,10 @@
             pltpu.SemaphoreType.DMA,
         ],
         compiler_params=pltpu.CompilerParams(
-            collective_id=0, has_side_effects=True, vmem_limit_bytes=64_000_000
+            collective_id=0, has_side_effects=True, vmem_limit_bytes=60_000_000
         ),
         name="exchange_attention",
     )(mem_ids.transpose(1, 2, 0), queries, keys, values, mem_keys, mem_values)
-    block = pl.BlockSpec((rows // 4, columns), lambda step: (step, 0))
-    return pl.pallas_call(
-        hand_over,
-        out_shape=jax.ShapeDtypeStruct((rows, columns), jnp.bfloat16),
-        grid=(4,),
-        in_specs=[block],
-        out_specs=block,
-        name="hand_over",
-    )(attended)
 
 
 def solution(mesh):

time: 190 us -> 187 us (0.984)
  Pallas kernels: 190 us -> 186 us
    pallas_call x2 -> x1, Pallas kernels: 190 us -> 186 us  [shards(): pl.pallas_call(functools.partial(kernel, devices, capacity), out_shape=pl...]
where the time goes in v2:
time: 187 us
  Pallas kernels  186 us (99%)
    pallas_call x1, Pallas kernels, shards(): pl.pallas_call(functools.partial(kernel, devices, capacity), out_shape=pl...  186 us

profile of v2, /device:TPU:1, one launch (start us, length us, event | category | flops | bytes accessed | tf_op | source)
XLA Modules:
  0.0 187.3 jit_solution(4017671296963459184)
XLA Ops:
  0.0 186.0 %exchange_attention.1 = bf16[256,4096]{1,0:T(8,128)(2,1)S(1)} custom-call(s32[2,2,32]{2,1,0:T(2,128)} %bitcast.1, bf16[256,4096]{1,0:T(8,128)(2,1)} %q_hbm.1, bf16[256,4096]{1,0:T(8,128)(2,1)} %k_hbm.1, bf16[256,4096]{1,0:T(8,128)(2,1)} %v_hbm.1, bf16[2,512,4096]{2,1,0:T(8,128)(2,1)} %mk_hbm.1, bf16[2,512,4096]{2,1,0:T(8,128)(2,1)} %mv_hbm.1), custom_call_target="tpu_custom_call" | custom-call | tf_op jit(solution)/shard_map/exchange_attention/pallas_call | solution.py:255
  186.0 1.3 copy.8
